TPU v7x, 256 devices: a whole 4x4x8 slice. The times are simulated.
256 devices in a mesh: client: 32 (over z_lo, y, core), mp: 8 (over x, z_hi).
Axes of the slice: x: 4, y: 4, z: 8 (z_hi: 2, z_lo: 4; z = z_hi * 4 + z_lo), core: 2. Of those that a mesh axis runs over, the one named last changes fastest.
Arguments:
- hidden: bfloat16 [32, 4, 128, 7168], P('client', None, None, 'mp'), may hold values from -6 to 6
- weight: bfloat16 [32, 7168, 2048], P('client', 'mp'), may hold values from -0.0625 to 0.0625
- target: bfloat16 [32, 4, 128, 2048], P('client', None, 'mp'), may hold values from -6 to 6
- router_prob: float32 [32, 4, 128], P('client', None, 'mp'), may hold values from 0.2 to 1
- routes: int32 [32, 4, 128, 2], P('client', None, 'mp'), may hold values from 0 to 7, all different within a row
- assign: int32 [32, 1], replicated, may hold values from 0 to 3
Outputs:
- merged_weight: bfloat16 [32, 7168, 2048], P('client', 'mp')
Inputs may be any that keep to these rules, and one draw needn't show every extreme that they name: `routes`: each token names two different experts; the given weights are those of expert 0. `assign`: every cluster has at least one client.
All inputs are finite; a program needn't handle non-finite values.
Results may differ from a plain program's by a relative error of at most 0.0044.
The roundings to bfloat16 on the way count: a program that leaves them out, or rounds other values in their place, can miss the bound.
Values may be sent and summed in bfloat16 or wider, within the bound.
A program may use at most 128 MiB of HBM per device.

v0:
```python
import jax
import jax.numpy as jnp
from jax import lax
from jax.sharding import PartitionSpec as P

D = 2048
FFW = 7168
NB = 4
CLUSTERS = 4


EPS = 1e-06
FLOOR = 0.1


def body(hidden, weight, target, router_prob, routes, assign):
    local_weight = weight[0]
    fisher = jnp.zeros(local_weight.shape, jnp.float32)
    for batch in range(NB):
        batch_hidden = hidden[0, batch]
        outputs = lax.psum_scatter(
            jnp.dot(batch_hidden, local_weight, preferred_element_type=jnp.float32),
            "mp",
            scatter_dimension=0,
            tiled=True,
        )
        token_weight = jnp.where(
            jnp.any(routes[0, batch] == 0, axis=-1), router_prob[0, batch], 0.0
        )
        grad_out = (
            token_weight[:, None] * (outputs - target[0, batch].astype(jnp.float32))
        ).astype(jnp.bfloat16)
        grad = lax.dot_general(
            batch_hidden,
            lax.all_gather(grad_out, "mp", axis=0, tiled=True),
            (((0,), (0,)), ((), ())),
            preferred_element_type=jnp.float32,
        )
        fisher = fisher + grad * grad
    total_fisher = lax.psum(jnp.sum(fisher), "mp")
    mean_fisher = total_fisher / (FFW * D)
    a_weight = (fisher / (mean_fisher + EPS) + FLOOR).astype(jnp.bfloat16)
    got_a, got_w = (
        lax.all_to_all(a_weight[None], "client", split_axis=1, concat_axis=0, tiled=True),
        lax.all_to_all(local_weight[None], "client", split_axis=1, concat_axis=0, tiled=True),
    )
    member_table = (assign[:, 0][:, None] == jnp.arange(CLUSTERS)[None, :]).astype(jnp.float32)
    a_float = got_a.astype(jnp.float32)
    weighted = a_float * got_w.astype(jnp.float32)
    num_part = jnp.einsum("sk,srd->krd", member_table, weighted, precision=lax.Precision.HIGHEST)
    den_part = jnp.einsum("sk,srd->krd", member_table, a_float, precision=lax.Precision.HIGHEST)
    merged = (num_part / den_part).astype(jnp.bfloat16)
    own_cluster = lax.dynamic_index_in_dim(
        assign[:, 0], lax.axis_index("client"), 0, keepdims=False
    )
    every_cluster = lax.all_gather(merged, "client", axis=1, tiled=True)
    result = lax.dynamic_index_in_dim(every_cluster, own_cluster, 0, keepdims=True)
    return result


def solution(mesh):
    placed = (
        P("client", None, None, "mp"),
        P("client", "mp", None),
        P("client", None, "mp", None),
        P("client", None, "mp"),
        P("client", None, "mp", None),
        P(),
    )
    return jax.shard_map(
        body, mesh=mesh, in_specs=placed, out_specs=P("client", "mp", None), check_vma=False
    )
```

profile of v0, /device:TPU:1, one launch (start us, length us, event | category | flops | bytes accessed | tf_op | source)
XLA Modules:
  0.0 917.2 jit_solution(14706498457414140986)
XLA Ops:
  6.5 0.0 copy-start.1
  6.5 0.0 reduce-scatter.11.cloned.1.call-start
  6.5 3.9 fusion.2
  10.5 0.0 reduce-scatter.11.cloned.1.call-update
  10.5 0.0 reduce-scatter.5.cloned.1.call-start
  10.5 3.9 fusion.8
  14.4 0.0 reduce-scatter.5.cloned.1.call-update
  14.5 0.0 reduce-scatter.7.cloned.1.call-start
  14.5 0.0 copy-done.1
  14.5 3.8 fusion.6
  18.3 0.0 reduce-scatter.7.cloned.1.call-update
  18.3 7.8 copy.31
  26.1 0.6 broadcast.41
  26.7 23.7 %reduce.10 = bf16[896,2048]{1,0:T(8,128)(2,1)} reduce(bf16[896,1,2048]{2,1,0:T(2,128)(2,1)} %bitcast.73, bf16[]{:T(256)} %broadcast.41), dimensions={1}, to_apply=%bitcast.72.reduce_sub_computation | reduce | bytes 7340034
  50.3 8.7 reshape.64
  59.1 0.0 copy-start.3
  59.1 0.0 copy-start.5
  59.1 10.4 %all-to-all-start.1 = ((bf16[32,2,28672]{2,1,0:T(2,128)(2,1)}), bf16[32,2,28672]{2,1,0:T(2,128)(2,1)}, u32[]{:S(2)}, u32[]{:S(2)}) async-start(bf16[32,2,28672]{2,1,0:T(2,128)(2,1)} %reshape.64), calls=%async_computation.5 | async-start | bytes 7340032 | tf_op jit(solution)/shard_map/all_to_all | solution.py:45
  69.4 0.0 reduce-scatter.9.cloned.1.call-start
  69.5 3.7 fusion.4
  73.2 0.0 reduce-scatter.9.cloned.1.call-update
  73.3 0.0 copy-done.3
  73.3 0.0 copy-done.5
  73.3 27.6 %reduce-scatter.11.cloned.1.call-done = f32[16,2048]{1,0:T(8,128)} async-done(((f32[128,2048]{1,0:T(8,128)}), f32[16,2048]{1,0:T(8,128)}) %reduce-scatter.11.cloned.1.call-update) | async-done | bytes 131088 | tf_op jit(solution)/shard_map/reduce_scatter | solution.py:21
  100.9 95.0 %reduce-scatter.5.cloned.1.call-done = f32[16,2048]{1,0:T(8,128)} async-done(((f32[128,2048]{1,0:T(8,128)}), f32[16,2048]{1,0:T(8,128)}) %reduce-scatter.5.cloned.1.call-update) | async-done | bytes 131088 | tf_op jit(solution)/shard_map/reduce_scatter | solution.py:21
  195.9 86.6 %reduce-scatter.7.cloned.1.call-done = f32[16,2048]{1,0:T(8,128)} async-done(((f32[128,2048]{1,0:T(8,128)}), f32[16,2048]{1,0:T(8,128)}) %reduce-scatter.7.cloned.1.call-update) | async-done | bytes 131088 | tf_op jit(solution)/shard_map/reduce_scatter | solution.py:21
  282.5 87.1 %reduce-scatter.9.cloned.1.call-done = f32[16,2048]{1,0:T(8,128)} async-done(((f32[128,2048]{1,0:T(8,128)}), f32[16,2048]{1,0:T(8,128)}) %reduce-scatter.9.cloned.1.call-update) | async-done | bytes 131088 | tf_op jit(solution)/shard_map/reduce_scatter | solution.py:21
  369.7 0.0 copy-done.2
  369.7 1.2 fusion.39
  370.9 41.3 %all_gather.17 = bf16[128,2048]{1,0:T(8,128)(2,1)S(1)} all-gather(bf16[16,2048]{1,0:T(8,128)(2,1)S(1)} %get-tuple-element.12), channel_id=1, replica_groups=mesh['client'=32,'mp'=8] {'mp'}, dimensions={0}, use_global_device_ids=true | all-gather | bytes 589824 | tf_op jit(solution)/shard_map/all_gather | solution.py:35
  412.1 42.5 %all_gather.16 = bf16[128,2048]{1,0:T(8,128)(2,1)S(1)} all-gather(bf16[16,2048]{1,0:T(8,128)(2,1)S(1)} %get-tuple-element.10), channel_id=1, replica_groups=mesh['client'=32,'mp'=8] {'mp'}, dimensions={0}, use_global_device_ids=true | all-gather | bytes 589824 | tf_op jit(solution)/shard_map/all_gather | solution.py:35
  454.6 42.9 %all_gather.15 = bf16[128,2048]{1,0:T(8,128)(2,1)S(1)} all-gather(bf16[16,2048]{1,0:T(8,128)(2,1)S(1)} %get-tuple-element.11), channel_id=1, replica_groups=mesh['client'=32,'mp'=8] {'mp'}, dimensions={0}, use_global_device_ids=true | all-gather | bytes 589824 | tf_op jit(solution)/shard_map/all_gather | solution.py:35
  497.5 41.5 %all_gather.18 = bf16[128,2048]{1,0:T(8,128)(2,1)S(1)} all-gather(bf16[16,2048]{1,0:T(8,128)(2,1)S(1)} %get-tuple-element.9), channel_id=1, replica_groups=mesh['client'=32,'mp'=8] {'mp'}, dimensions={0}, use_global_device_ids=true | all-gather | bytes 589824 | tf_op jit(solution)/shard_map/all_gather | solution.py:35
  539.0 1.1 fusion.21
  540.2 1.1 fusion.24
  541.3 1.1 fusion.27
  542.5 4.9 fusion.51
  547.3 21.0 %psum.7 = f32[]{:T(128)} all-reduce(f32[]{:T(128)} %get-tuple-element.17), channel_id=1, replica_groups=mesh['client'=32,'mp'=8] {'mp'}, use_global_device_ids=true, to_apply=%region_9.10 | all-reduce | flops 1 | bytes 8 | tf_op jit(solution)/shard_map/psum | solution.py:40
  569.0 5.7 fusion.12
  574.7 18.1 %copy.15 = bf16[1,896,2048]{2,0,1:T(2,128)(2,1)} copy(bf16[1,896,2048]{1,2,0:T(8,128)(2,1)} %fusion.12) | data formatting | bytes 7340032 | tf_op jit(solution)/shard_map/broadcast_in_dim | solution.py:44
  592.8 23.7 %reduce.9 = bf16[896,2048]{1,0:T(8,128)(2,1)} reduce(bf16[896,1,2048]{2,1,0:T(2,128)(2,1)} %bitcast.74, bf16[]{:T(256)} %broadcast.41), dimensions={1}, to_apply=%bitcast.59.reduce_sub_computation | reduce | bytes 7340034
  616.5 8.7 reshape.62
  625.2 0.0 all-to-all-done.1
  625.2 38.2 %all-to-all-start = ((bf16[32,2,28672]{2,1,0:T(2,128)(2,1)}), bf16[32,2,28672]{2,1,0:T(2,128)(2,1)}, u32[]{:S(2)}, u32[]{:S(2)}) async-start(bf16[32,2,28672]{2,1,0:T(2,128)(2,1)} %reshape.62), calls=%async_computation.4 | async-start | bytes 7340032 | tf_op jit(solution)/shard_map/all_to_all | solution.py:44
  663.4 0.0 all-gather.2.cloned.1.call-start
  663.4 19.3 %reshape.65 = bf16[896,1,2048]{2,1,0:T(2,128)(2,1)} reshape(bf16[32,2,28672]{2,1,0:T(2,128)(2,1)} %all-to-all-done.1) | data formatting | bytes 7340032
  682.7 24.4 %convert_reduce_fusion = f32[896,2048]{1,0:T(8,128)} fusion(bf16[896,1,2048]{2,1,0:T(2,128)(2,1)} %reshape.65), kind=kLoop, calls=%fused_computation.4 | loop fusion | flops 1835008 | bytes 11010048 | tf_op jit(solution)/shard_map/convert_element_type | solution.py:49
  707.1 8.0 reshape.58
  715.1 30.2 %all-to-all-done = bf16[32,2,28672]{2,1,0:T(2,128)(2,1)} async-done(((bf16[32,2,28672]{2,1,0:T(2,128)(2,1)}), bf16[32,2,28672]{2,1,0:T(2,128)(2,1)}, u32[]{:S(2)}, u32[]{:S(2)}) %all-to-all-start) | async-done | bytes 3670048 | tf_op jit(solution)/shard_map/all_to_all | solution.py:44
  745.3 19.3 %reshape.63 = bf16[896,1,2048]{2,1,0:T(2,128)(2,1)} reshape(bf16[32,2,28672]{2,1,0:T(2,128)(2,1)} %all-to-all-done) | data formatting | bytes 7340032
  764.6 23.6 %bitcast_reduce_fusion = bf16[896,2048]{1,0:T(8,128)(2,1)} fusion(bf16[896,1,2048]{2,1,0:T(2,128)(2,1)} %reshape.63), kind=kLoop, calls=%fused_computation.65 | loop fusion | bytes 7340032 | tf_op jit(solution)/shard_map/all_to_all | solution.py:44
  788.2 5.9 all_to_all.7
  794.1 0.0 copy-start
  794.1 0.0 copy-start.4
  794.1 6.0 convert_multiply_fusion
  800.1 0.0 copy-done
  800.1 0.0 copy-done.4
  800.2 4.0 fusion.10
  804.2 7.7 fusion.16
  811.9 0.0 all-gather.2.cloned.1.call-update
  811.9 0.6 constant_dynamic-slice_fusion.1
  814.5 82.3 %all-gather.2.cloned.1.call-done = bf16[4,896,2048]{2,0,1:T(4,128)(2,1)} async-done(((bf16[4,28,2048]{2,0,1:T(4,128)(2,1)}), bf16[4,896,2048]{2,0,1:T(4,128)(2,1)}) %all-gather.2.cloned.1.call-update) | async-done | bytes 14680080 | tf_op jit(solution)/shard_map/all_gather | solution.py:56
  896.8 9.3 %constant_dynamic-slice_fusion = bf16[1,896,2048]{2,0,1:T(2,128)(2,1)S(1)} fusion(bf16[4,896,2048]{2,0,1:T(4,128)(2,1)} %all-gather.2.cloned.1.call-done, s32[]{:T(128)S(6)} %select_n.42), kind=kLoop, calls=%fused_computation.62 | loop fusion | bytes 7340036 | tf_op jit(solution)/shard_map/jit(dynamic_index_in_dim)/dynamic_slice | solution.py:57
  906.1 4.1 copy.19
  (3 shorter events, 0.0 us)
Async XLA Ops:
  6.5 8.0 copy-start.1
  6.5 94.4 %reduce-scatter.11.cloned.1.call-start = ((), (), s32[]{:S(2)}) async-start(), calls=%async_computation.9 | async-start | bytes 1179648 | tf_op jit(solution)/shard_map/reduce_scatter | solution.py:21
  10.5 185.4 %reduce-scatter.5.cloned.1.call-start = ((), (), s32[]{:S(2)}) async-start(), calls=%async_computation.6 | async-start | bytes 1179648 | tf_op jit(solution)/shard_map/reduce_scatter | solution.py:21
  14.5 268.1 %reduce-scatter.7.cloned.1.call-start = ((), (), s32[]{:S(2)}) async-start(), calls=%async_computation.7 | async-start | bytes 1179648 | tf_op jit(solution)/shard_map/reduce_scatter | solution.py:21
  59.1 14.2 %copy-start.3 = (s32[1,4,16,2]{2,3,1,0:T(2,128)S(1)}, s32[1,4,16,2]{2,3,1,0:T(2,128)}, u32[]{:S(2)}) copy-start(s32[1,4,16,2]{2,3,1,0:T(2,128)} %param.10) | copy-start | bytes 1540
  59.1 14.2 %copy-start.5 = (f32[1,4,16]{2,1,0:T(4,128)S(1)}, f32[1,4,16]{2,1,0:T(4,128)}, u32[]{:S(2)}) copy-start(f32[1,4,16]{2,1,0:T(4,128)} %param.9) | copy-start | bytes 772
  59.1 310.6 %copy-start.2 = (bf16[1,4,16,2048]{3,2,1,0:T(8,128)(2,1)S(1)}, bf16[1,4,16,2048]{3,2,1,0:T(8,128)(2,1)}, u32[]{:S(2)}) copy-start(bf16[1,4,16,2048]{3,2,1,0:T(8,128)(2,1)} %param.8) | copy-start | bytes 786436
  59.1 566.1 %all-to-all-start.1 = ((bf16[32,2,28672]{2,1,0:T(2,128)(2,1)}), bf16[32,2,28672]{2,1,0:T(2,128)(2,1)}, u32[]{:S(2)}, u32[]{:S(2)}) async-start(bf16[32,2,28672]{2,1,0:T(2,128)(2,1)} %reshape.64), calls=%async_computation.5 | async-start | bytes 7340032 | tf_op jit(solution)/shard_map/all_to_all | solution.py:45
  69.4 300.2 %reduce-scatter.9.cloned.1.call-start = ((), (), s32[]{:S(2)}) async-start(), calls=%async_computation.8 | async-start | bytes 1179648 | tf_op jit(solution)/shard_map/reduce_scatter | solution.py:21
  625.2 120.1 %all-to-all-start = ((bf16[32,2,28672]{2,1,0:T(2,128)(2,1)}), bf16[32,2,28672]{2,1,0:T(2,128)(2,1)}, u32[]{:S(2)}, u32[]{:S(2)}) async-start(bf16[32,2,28672]{2,1,0:T(2,128)(2,1)} %reshape.62), calls=%async_computation.4 | async-start | bytes 7340032 | tf_op jit(solution)/shard_map/all_to_all | solution.py:44
  663.4 233.5 %all-gather.2.cloned.1.call-start = ((), (), s32[]{:S(2)}) async-start(), calls=%async_computation.10 | async-start | bytes 15138816 | tf_op jit(solution)/shard_map/all_gather | solution.py:56
  794.1 6.0 copy-start
  794.1 6.0 copy-start.4
Sparse Core Ops, SparseCore 0:
  11.3 89.5 reduce-scatter.10
  105.3 90.5 reduce-scatter.4
  199.8 82.6 reduce-scatter.6
  286.8 82.7 reduce-scatter.8
  812.1 84.7 all-gather.1
where the time goes:
time: 926 us; the launch traced here: 917 us
  waiting for transfers between devices  409 us (44%)
  blocking collectives  189 us (20%)
  local copies, waits for them, and re-layouts  134 us (14%)
  other arithmetic  84.6 us (9%)
  starting transfers between devices  48.7 us (5%)
  matrix products  35.4 us (4%)
  between operations  16.3 us (2%)
    reduce_scatter x4, waiting for transfers between devices, body(): lax.psum_scatter(jnp.dot(batch_hidden, local_weight, preferred_element_ty...  296 us
    all_gather x4, blocking collectives, body(): lax.all_gather(grad_out, 'mp', axis=0, tiled=True)  168 us
    all_gather x1, waiting for transfers between devices, body(): every_cluster = lax.all_gather(merged, 'client', axis=1, tiled=True)  82.3 us
    unnamed x18, local copies, waits for them, and re-layouts  64.4 us
    unnamed x2, other arithmetic  47.4 us
    all_to_all x1, starting transfers between devices, body(): lax.all_to_all(a_weight[None], 'client', split_axis=1, concat_axis=0, til...  38.2 us
    all_to_all x1, waiting for transfers between devices, body(): lax.all_to_all(a_weight[None], 'client', split_axis=1, concat_axis=0, til...  30.2 us
    all_to_all x2, local copies, waits for them, and re-layouts, body(): lax.all_to_all(a_weight[None], 'client', split_axis=1, concat_axis=0, til...  29.5 us
  transfers between devices with their start and end apart: 7, of which 6 were waited for; matrix products, arithmetic and copies ran while one was open for 19% of the time, Pallas kernels for 0%

commit v1 on v0

v1 whole, which is shorter than its diff:
```python
import functools

import jax
import jax.numpy as jnp
from jax import lax
from jax.experimental import pallas as pl
from jax.experimental.pallas import tpu as pltpu
from jax.sharding import PartitionSpec as P

D = 2048
FFW = 7168
NB = 4
CLUSTERS = 4
EPS = 1e-06
FLOOR = 0.1

F = 896
TOK = 128
OWN = 112
G16 = 16
NG = OWN // G16
NS = 2 * NG
HALF = D // 2
QUART = D // 4
WMAX = 0.0625
CODE = 32760.0 / WMAX

MESH = pl.DeviceIdType.MESH
f32 = jnp.float32
bf16 = jnp.bfloat16


def rcopy(src, dst, send, recv, device):
    return pltpu.make_async_remote_copy(
        src_ref=src, dst_ref=dst, send_sem=send, recv_sem=recv, device_id=device, device_id_type=MESH
    )


def kernel(
    hid, w, tgt, tw, mask, cluster, out,
    hid_t, y_f32, own, y_send, y_recv, z_send, z_recv, grad_out, fisher, sums, a_send, a_recv, w_recv,
    num, den, m_send, d_send, m_recv, d_recv, merged, picked,
    w_s, w_r, y_s, y_r, z_s, z_r, zg_s, zg_r, xg_s, xg_r, t_s, t_r, a_s, a_r, c_s, c_r, b_s, b_r, o_s, o_r, l_s,
):
    c = lax.axis_index("client")
    m = lax.axis_index("mp")
    zl, q = c // 8, c % 8
    xx, zh = m // 2, m % 2

    def plane(k):
        return (zl * 8 + k, m)

    def group(k):
        return (c, k)

    def line(k):
        return (k * 8 + q, m)

    barrier = pltpu.get_barrier_semaphore()
    for k in range(1, 8):
        pl.semaphore_signal(barrier, inc=1, device_id=plane((q + k) % 8), device_id_type=MESH)
        pl.semaphore_signal(barrier, inc=1, device_id=group((m + k) % 8), device_id_type=MESH)

    for k in (1, 3):
        pl.semaphore_signal(barrier, inc=1, device_id=line((zl + k) % 4), device_id_type=MESH)
    pl.semaphore_wait(barrier, 16)

    def w_copy(k, slot):
        rows = pl.ds(pl.multiple_of(k * OWN, 16), OWN)
        return rcopy(w.at[rows], w_recv.at[slot], w_s.at[k], w_r.at[slot], plane(k))

    def y_copy(b, k, slot):
        rows = pl.ds(pl.multiple_of(k * 32, 32), 32)
        return rcopy(
            y_send.at[b, rows], y_recv.at[b, slot], y_s.at[b, k], y_r.at[b, slot], group(k * 2 + zh)
        )

    def y_batch(b, _):
        for n in range(4):
            cols = pl.ds(n * QUART, QUART)
            y_f32[:, cols] = jnp.dot(hid[b], w[:, cols], preferred_element_type=f32)
            y_send[b, :, cols] = y_f32[:, cols].astype(bf16)
        own[b] = y_f32[pl.ds(pl.multiple_of(xx * 32, 32), 32), :]
        for k in range(1, 4):
            y_copy(b, (xx + k) % 4, xx).start()
        return 0

    lax.fori_loop(0, NB, y_batch, 0)

    for k in range(1, 8):
        w_copy((q + k) % 8, q).start()

    def prepare(b, _):
        hid_t[b] = hid[b].T
        return 0

    lax.fori_loop(0, NB, prepare, 0)

    def clear(r, _):
        rows = pl.ds(pl.multiple_of(r * 16, 16), 16)
        fisher[rows] = jnp.zeros((16, D), f32)
        return 0

    lax.fori_loop(0, F // 16, clear, 0)
    sums[m] = jnp.zeros((8, 256), f32)

    def keep_w(r, _):
        w_recv[q, pl.ds(pl.multiple_of(r * 16, 16), 16)] = w[pl.ds(pl.multiple_of(q * OWN + r * 16, 16), 16)]
        return 0

    lax.fori_loop(0, NG, keep_w, 0)

    mine = pl.ds(pl.multiple_of(m * 16, 16), 16)
    theirs = pl.ds(pl.multiple_of((xx * 2 + 1 - zh) * 16, 16), 16)
    partner = group(xx * 2 + 1 - zh)

    def z_copy(b):
        return rcopy(z_send.at[b], z_recv.at[b], z_s.at[b], z_r.at[b], partner)

    def zg_copy(b, rows):
        return rcopy(grad_out.at[b, rows], grad_out.at[b, rows], zg_s.at[b], zg_r.at[b], partner)

    def xg_copy(b, k, block):
        rows = pl.ds(pl.multiple_of(block * 32, 32), 32)
        return rcopy(
            grad_out.at[b, rows], grad_out.at[b, rows], xg_s.at[b, k], xg_r.at[b, block], group(k * 2 + zh)
        )

    def step_x(b):
        total = own[b]
        for k in range(1, 4):
            slot = (xx + k) % 4
            y_copy(b, slot, slot).wait_recv()
            total = total + y_recv[b, slot].astype(f32)
        own[b] = total
        z_send[b] = own[b, pl.ds(pl.multiple_of((1 - zh) * 16, 16), 16)].astype(bf16)
        z_copy(b).start()

    def step_z(b):
        z_copy(b).wait_recv()
        y = own[b, pl.ds(pl.multiple_of(zh * 16, 16), 16)] + z_recv[b].astype(f32)
        grad_out[b, mine] = (tw[b][:, :1] * (y - tgt[b].astype(f32))).astype(bf16)
        zg_copy(b, mine).start()

    def step_g(b):
        zg_copy(b, theirs).wait_recv()
        for k in range(1, 4):
            xg_copy(b, (xx + k) % 4, xx).start()

    def step_f(b):
        for k in range(1, 4):
            slot = (xx + k) % 4
            xg_copy(b, slot, slot).wait_recv()

        def tile(n, _):
            cols = pl.ds(pl.multiple_of(n * 256, 256), 256)
            g = jnp.dot(hid_t[b], grad_out[b, :, cols], preferred_element_type=f32)
            g = g * g
            fisher[:, cols] += g
            sums[m] += g.reshape(F // 8, 8, 256).sum(0)
            return 0

        lax.fori_loop(0, D // 256, tile, 0)

    def mp_step(t, _):
        pl.when(t < NB)(lambda: step_x(t))
        pl.when((t >= 1) & (t < NB + 1))(lambda: step_z(t - 1))
        pl.when((t >= 2) & (t < NB + 2))(lambda: step_g(t - 2))
        pl.when(t >= 3)(lambda: step_f(t - 3))
        return 0

    lax.fori_loop(0, NB + 3, mp_step, 0)

    def t_copy(k, slot):
        return rcopy(sums.at[slot], sums.at[slot], t_s.at[k], t_r.at[slot], group(k))

    for k in range(1, 8):
        t_copy((m + k) % 8, m).start()
    for k in range(1, 8):
        slot = (m + k) % 8
        t_copy(slot, slot).wait_recv()
    total = sums[0]
    for k in range(1, 8):
        total = total + sums[k]
    mean = jnp.sum(total) / (FFW * D)
    scale = 1.0 / jnp.full((8, 128), mean + EPS, f32)
    scale = scale[:1, :1]

    def a_copy(r, k, slot):
        src = pl.ds(pl.multiple_of(k * OWN + r * 16, 16), 16)
        dst = pl.ds(pl.multiple_of(r * 16, 16), 16)
        return rcopy(a_send.at[src], a_recv.at[slot, dst], a_s.at[k, r], a_r.at[slot, r], plane(k))

    def a_group(r, _):
        for k in range(1, 8):
            peer = (q + k) % 8
            rows = pl.ds(pl.multiple_of(peer * OWN + r * 16, 16), 16)
            a_send[rows] = (fisher[rows] * scale + FLOOR).astype(bf16)
            a_copy(r, peer, q).start()
        rows = pl.ds(pl.multiple_of(q * OWN + r * 16, 16), 16)
        a_recv[q, pl.ds(pl.multiple_of(r * 16, 16), 16)] = (fisher[rows] * scale + FLOOR).astype(bf16)
        return 0

    lax.fori_loop(0, NG, a_group, 0)

    for k in range(1, 8):
        slot = (q + k) % 8
        w_copy(slot, slot).wait_recv()

    def where(j):
        r, h = j // 2, j % 2
        return pl.ds(pl.multiple_of(r * 16, 16), 16), r, h

    def own_sums(j):
        rows, r, h = where(j)

        @pl.when(h == 0)
        def _():
            for k in range(1, 8):
                slot = (q + k) % 8
                a_copy(r, slot, slot).wait_recv()

        def tile(n, _):
            cols = pl.ds(pl.multiple_of(h * HALF + n * 256, 256), 256)
            nums = [jnp.zeros((16, 256), f32)] * CLUSTERS
            dens = [jnp.zeros((16, 256), f32)] * CLUSTERS
            for s in range(8):
                a = a_recv[s, rows, cols].astype(f32)
                aw = a * w_recv[s, rows, cols].astype(f32)
                for k in range(CLUSTERS):
                    member = mask[zl * 8 + s, k]
                    nums[k] = nums[k] + member * aw
                    dens[k] = dens[k] + member * a
            for k in range(CLUSTERS):
                num[k, rows, cols] = nums[k]
                den[k, rows, cols] = dens[k]
            return 0

        lax.fori_loop(0, HALF // 256, tile, 0)

    def columns(way, h):
        return pl.ds(pl.multiple_of(h * HALF + way * QUART, QUART), QUART)

    def m_copy(way, j, peer):
        return rcopy(m_send.at[way, j], m_recv.at[way, j], c_s.at[way, j, 0], c_r.at[way, j, 0], peer)

    def d_copy(way, j, peer):
        return rcopy(d_send.at[way, j], d_recv.at[way, j], c_s.at[way, j, 1], c_r.at[way, j, 1], peer)

    def b_copy(way, j, peer):
        rows, _, h = where(j)
        part = merged.at[:, rows, columns(way, h)]
        return rcopy(part, part, b_s.at[way, j], b_r.at[way, j], peer)

    def ends(way):
        if way == 0:
            return zl, line((zl + 1) % 4), line((zl + 3) % 4)
        return 3 - zl, line((zl + 3) % 4), line((zl + 1) % 4)

    def chain(way, i):
        hop, ahead, behind = ends(way)
        j = i - hop

        @pl.when((j >= 0) & (j < NS))
        def _():
            rows, _, h = where(j)
            cols = columns(way, h)

            @pl.when(hop > 0)
            def _():
                m_copy(way, j, behind).wait_recv()
                d_copy(way, j, behind).wait_recv()
                for k in range(CLUSTERS):
                    d = d_recv[way, j, k].astype(f32)
                    v = m_recv[way, j, k].astype(jnp.int32).astype(f32) * (1.0 / CODE)
                    num[k, rows, cols] += v * d
                    den[k, rows, cols] += d

            @pl.when(hop < 3)
            def _():
                for k in range(CLUSTERS):
                    d = den[k, rows, cols]
                    v = num[k, rows, cols] / jnp.maximum(d, 0.0625)
                    m_send[way, j, k] = jnp.round(v * CODE).astype(jnp.int32).astype(jnp.int16)
                    d_send[way, j, k] = d.astype(bf16)
                m_copy(way, j, ahead).start()
                d_copy(way, j, ahead).start()

            @pl.when(hop == 3)
            def _():
                for k in range(CLUSTERS):
                    merged[k, rows, cols] = (num[k, rows, cols] / den[k, rows, cols]).astype(bf16)
                b_copy(way, j, behind).start()

    def back(way, i):
        hop, ahead, behind = ends(way)
        j = i - (6 - hop)

        @pl.when((j >= 0) & (j < NS) & (hop < 3))
        def _():
            b_copy(way, j, ahead).wait_recv()

            @pl.when(hop > 0)
            def _():
                b_copy(way, j, behind).start()

    def o_copy(j, k, owner):
        rows, r, h = where(j)
        cols = pl.ds(pl.multiple_of(h * HALF, HALF), HALF)
        dst = out.at[pl.ds(pl.multiple_of(owner * OWN + r * 16, 16), 16), cols]
        return rcopy(picked.at[k, rows, cols], dst, o_s.at[k, j], o_r.at[owner, j], plane(k))

    def l_copy(j):
        rows, r, h = where(j)
        cols = pl.ds(pl.multiple_of(h * HALF, HALF), HALF)
        dst = out.at[pl.ds(pl.multiple_of(q * OWN + r * 16, 16), 16), cols]
        return pltpu.make_async_copy(picked.at[q, rows, cols], dst, l_s.at[j])

    def scatter(j):
        rows, _, h = where(j)
        cols = pl.ds(pl.multiple_of(h * HALF, HALF), HALF)
        for k in range(8):
            peer = (q + k) % 8
            own_cluster = cluster[zl * 8 + peer, 0]
            v = merged[0, rows, cols]
            for n in range(1, CLUSTERS):
                v = jnp.where(own_cluster == n, merged[n, rows, cols], v)
            picked[peer, rows, cols] = v
            if k == 0:
                l_copy(j).start()
            else:
                o_copy(j, peer, q).start()

    def merge_step(i, _):
        pl.when(i < NS)(lambda: own_sums(i))
        chain(0, i)
        chain(1, i)
        back(0, i)
        back(1, i)
        pl.when(i >= 6)(lambda: scatter(i - 6))
        return 0

    lax.fori_loop(0, NS + 6, merge_step, 0)

    def last_out(j, _):
        l_copy(j).wait()
        for k in range(1, 8):
            peer = (q + k) % 8
            o_copy(j, peer, peer).wait_recv()
            o_copy(j, peer, q).wait_send()
        for way in range(2):
            hop, ahead, behind = ends(way)

            @pl.when(hop < 3)
            def _():
                m_copy(way, j, ahead).wait_send()
                d_copy(way, j, ahead).wait_send()

            @pl.when(hop > 0)
            def _():
                b_copy(way, j, behind).wait_send()
        return 0

    lax.fori_loop(0, NS, last_out, 0)

    def last_a(r, _):
        for k in range(1, 8):
            a_copy(r, (q + k) % 8, q).wait_send()
        return 0

    lax.fori_loop(0, NG, last_a, 0)
    for k in range(1, 8):
        w_copy((q + k) % 8, q).wait_send()
        t_copy((m + k) % 8, m).wait_send()

    def last_mp(b, _):
        for k in range(1, 4):
            y_copy(b, (xx + k) % 4, xx).wait_send()
            xg_copy(b, (xx + k) % 4, xx).wait_send()
        z_copy(b).wait_send()
        zg_copy(b, mine).wait_send()
        return 0

    lax.fori_loop(0, NB, last_mp, 0)


def body(hidden, weight, target, router_prob, routes, assign):
    token_weight = jnp.where(jnp.any(routes[0] == 0, axis=-1), router_prob[0], 0.0)
    token_weight = jnp.broadcast_to(token_weight[:, :, None], (NB, 16, 128))
    member = (assign == jnp.arange(CLUSTERS)[None, :]).astype(f32)
    vmem = pl.BlockSpec(memory_space=pltpu.VMEM)
    smem = pl.BlockSpec(memory_space=pltpu.SMEM)
    V, S = pltpu.VMEM, pltpu.SemaphoreType.DMA
    result = pl.pallas_call(
        kernel,
        out_shape=jax.ShapeDtypeStruct((F, D), bf16),
        in_specs=[vmem, vmem, vmem, vmem, smem, smem],
        out_specs=pl.BlockSpec(memory_space=pl.ANY),
        scratch_shapes=[
            V((NB, F, TOK), bf16),
            V((TOK, D), f32),
            V((NB, 32, D), f32),
            V((NB, TOK, D), bf16),
            V((NB, 4, 32, D), bf16),
            V((NB, 16, D), bf16),
            V((NB, 16, D), bf16),
            V((NB, TOK, D), bf16),
            V((F, D), f32),
            V((8, 8, 256), f32),
            V((F, D), bf16),
            V((8, OWN, D), bf16),
            V((8, OWN, D), bf16),
            V((CLUSTERS, OWN, D), f32),
            V((CLUSTERS, OWN, D), f32),
            V((2, NS, CLUSTERS, G16, QUART), jnp.int16),
            V((2, NS, CLUSTERS, G16, QUART), bf16),
            V((2, NS, CLUSTERS, G16, QUART), jnp.int16),
            V((2, NS, CLUSTERS, G16, QUART), bf16),
            V((CLUSTERS, OWN, D), bf16),
            V((8, OWN, D), bf16),
            S((8,)), S((8,)),
            S((NB, 4)), S((NB, 4)),
            S((NB,)), S((NB,)),
            S((NB,)), S((NB,)),
            S((NB, 4)), S((NB, 4)),
            S((8,)), S((8,)),
            S((8, NG)), S((8, NG)),
            S((2, NS, 2)), S((2, NS, 2)),
            S((2, NS)), S((2, NS)),
            S((8, NS)), S((8, NS)),
            S((NS,)),
        ],
        compiler_params=pltpu.CompilerParams(
            collective_id=0, has_side_effects=True, vmem_limit_bytes=62 << 20
        ),
        cost_estimate=pl.CostEstimate(flops=4_000_000_000, bytes_accessed=12_000_000, transcendentals=0),
    )(hidden[0], weight[0], target[0], token_weight, member, assign)
    return result[None]


def solution(mesh):
    placed = (
        P("client", None, None, "mp"),
        P("client", "mp", None),
        P("client", None, "mp", None),
        P("client", None, "mp"),
        P("client", None, "mp", None),
        P(),
    )
    return jax.shard_map(
        body, mesh=mesh, in_specs=placed, out_specs=P("client", "mp", None), check_vma=False
    )
```

time: 926 us -> 182 us (0.20)
  waiting for transfers between devices: 409 us -> 0 us
  blocking collectives: 189 us -> 0 us
  Pallas kernels: 0 us -> 172 us
  local copies, waits for them, and re-layouts: 134 us -> 6.39 us
  other arithmetic: 84.6 us -> 2.71 us
  starting transfers between devices: 48.7 us -> 0 us
  matrix products: 35.4 us -> 0 us
  between operations: 16.3 us -> 0.01 us
    reduce_scatter x4 -> x0, waiting for transfers between devices: 296 us -> none  [body(): lax.psum_scatter(jnp.dot(batch_hidden, local_weight, preferred_element_ty...]
    pallas_call x0 -> x1, Pallas kernels: none -> 172 us  [body(): pl.pallas_call(kernel, out_shape=jax.ShapeDtypeStruct((F, D), bf16), in_s...]
    all_gather x4 -> x0, blocking collectives: 168 us -> none  [body(): lax.all_gather(grad_out, 'mp', axis=0, tiled=True)]
    all_gather x1 -> x0, waiting for transfers between devices: 82.3 us -> none  [body(): every_cluster = lax.all_gather(merged, 'client', axis=1, tiled=True)]
    unnamed x18 -> x2, local copies, waits for them, and re-layouts: 64.4 us -> 5.71 us
    all_to_all x2 -> x0, starting transfers between devices: 48.5 us -> none  [the longest x1 38.2 us: body(): lax.all_to_all(a_weight[None], 'client', split_axis=1, concat_axis=0, til...]
    unnamed x2 -> x0, other arithmetic: 47.4 us -> none
    dot_general x10 -> x0, matrix products: 35.4 us -> none  [the longest x4 15.3 us: body(): jnp.dot(batch_hidden, local_weight, preferred_element_type=jnp.float32)]
  transfers between devices with their start and end apart: 7 -> 0, of which waited for: 6 -> 0; matrix products, arithmetic and copies ran while one was open for 19% -> 0% of each run, Pallas kernels for 0% -> 0%
where the time goes in v1:
time: 182 us
  Pallas kernels  172 us (95%)
  local copies, waits for them, and re-layouts  6.39 us (4%)
  other arithmetic  2.71 us (1%)
    pallas_call x1, Pallas kernels, body(): pl.pallas_call(kernel, out_shape=jax.ShapeDtypeStruct((F, D), bf16), in_s...  172 us
    unnamed x2, local copies, waits for them, and re-layouts  5.71 us

profile of v1, /device:TPU:1, one launch (start us, length us, event | category | flops | bytes accessed | tf_op | source)
XLA Modules:
  0.0 181.5 jit_solution(17224118482615799156)
XLA Ops:
  0.0 0.7 compare_reduce_fusion
  0.7 0.7 bitcast_select_fusion
  1.4 1.3 fusion.mask
  2.7 1.3 copy.7.cluster
  4.0 0.7 broadcast_in_dim.15.tw
  4.7 172.4 %shard_map.64 = bf16[896,2048]{1,0:T(8,128)(2,1)} custom-call(bf16[4,128,896]{2,1,0:T(8,128)(2,1)} %bitcast.10, bf16[896,2048]{1,0:T(8,128)(2,1)} %bitcast.9, bf16[4,16,2048]{2,1,0:T(8,128)(2,1)} %bitcast.11, f32[4,16,128]{2,1,0:T(8,128)} %broadcast_in_dim.15.tw, f32[32,4]{1,0:T(8,128)} %fusion.mask, s32[32,1]{1,0:T(8,128)} %copy.7.cluster), custom_call_target="tpu_custom_call" | custom-call | flops 4000000000 | bytes 12000000 | tf_op jit(solution)/shard_map/pallas_call | solution.py:394
  177.1 4.4 %copy.9 = bf16[1,896,2048]{2,1,0:T(8,128)(2,1)} copy(bf16[1,896,2048]{2,1,0:T(8,128)(2,1)} %bitcast.7) | data formatting | bytes 7340032

commit v2 on v1

--- a/solution.py
+++ b/solution.py
@@ -19,11 +19,17 @@
 OWN = 112
 G16 = 16
 NG = OWN // G16
-NS = 2 * NG
-HALF = D // 2
+SPLIT = 4
+NS = SPLIT * NG
+WIDE = D // SPLIT
+HALF = WIDE // 2
+LAG = 2
 QUART = D // 4
 WMAX = 0.0625
 CODE = 32760.0 / WMAX
+LOW = 0.0625
+MID = 9.0
+STEP = 11.8 / 32760.0
 
 MESH = pl.DeviceIdType.MESH
 f32 = jnp.float32
@@ -37,10 +43,10 @@
 
 
 def kernel(
-    hid, w, tgt, tw, mask, cluster, out,
-    hid_t, y_f32, own, y_send, y_recv, z_send, z_recv, grad_out, fisher, sums, a_send, a_recv, w_recv,
-    num, den, m_send, d_send, m_recv, d_recv, merged, picked,
-    w_s, w_r, y_s, y_r, z_s, z_r, zg_s, zg_r, xg_s, xg_r, t_s, t_r, a_s, a_r, c_s, c_r, b_s, b_r, o_s, o_r, l_s,
+    hid_in, w_in, tgt, prob, routes, cluster, out,
+    hid, w, tw, hid_t, y_f32, own, y_send, y_recv, z_send, z_recv, grad_out, fisher, sums, a_send, a_recv, w_recv,
+    num, den, c_send, c_recv, merged, picked,
+    in_s, w_s, w_r, y_s, y_r, z_s, z_r, zg_s, zg_r, xg_s, xg_r, t_s, t_r, a_s, a_r, c_s, c_r, b_s, b_r, o_s, o_r, l_s,
 ):
     c = lax.axis_index("client")
     m = lax.axis_index("mp")
@@ -63,7 +69,19 @@
 
     for k in (1, 3):
         pl.semaphore_signal(barrier, inc=1, device_id=line((zl + k) % 4), device_id_type=MESH)
-    pl.semaphore_wait(barrier, 16)
+    load_hid = pltpu.make_async_copy(hid_in, hid, in_s.at[0])
+    load_w = pltpu.make_async_copy(w_in, w, in_s.at[1])
+    load_hid.start()
+    load_w.start()
+
+    eye = lax.broadcasted_iota(jnp.int32, (16, 16), 0) == lax.broadcasted_iota(jnp.int32, (16, 16), 1)
+    for b in range(NB):
+        chosen = jnp.max(jnp.where(routes[b] == 0, 1.0, 0.0), axis=0, keepdims=True) > 0
+        row = jnp.where(chosen, prob[b : b + 1, :], 0.0)
+        column = jnp.sum(jnp.where(eye, jnp.broadcast_to(row, (16, 16)), 0.0), axis=1, keepdims=True)
+        tw[b] = jnp.broadcast_to(column, (16, 128))
+    load_hid.wait()
+    load_w.wait()
 
     def w_copy(k, slot):
         rows = pl.ds(pl.multiple_of(k * OWN, 16), OWN)
@@ -81,6 +99,11 @@
             y_f32[:, cols] = jnp.dot(hid[b], w[:, cols], preferred_element_type=f32)
             y_send[b, :, cols] = y_f32[:, cols].astype(bf16)
         own[b] = y_f32[pl.ds(pl.multiple_of(xx * 32, 32), 32), :]
+
+        @pl.when(b == 0)
+        def _():
+            pl.semaphore_wait(barrier, 16)
+
         for k in range(1, 4):
             y_copy(b, (xx + k) % 4, xx).start()
         return 0
@@ -189,7 +212,7 @@
     def a_copy(r, k, slot):
         src = pl.ds(pl.multiple_of(k * OWN + r * 16, 16), 16)
         dst = pl.ds(pl.multiple_of(r * 16, 16), 16)
-        return rcopy(a_send.at[src], a_recv.at[slot, dst], a_s.at[k, r], a_r.at[slot, r], plane(k))
+        return rcopy(a_send.at[src], a_recv.at[slot, dst], a_s.at[k], a_r.at[slot, r], plane(k))
 
     def a_group(r, _):
         for k in range(1, 8):
@@ -208,7 +231,7 @@
         w_copy(slot, slot).wait_recv()
 
     def where(j):
-        r, h = j // 2, j % 2
+        r, h = j // SPLIT, j % SPLIT
         return pl.ds(pl.multiple_of(r * 16, 16), 16), r, h
 
     def own_sums(j):
@@ -220,37 +243,32 @@
                 slot = (q + k) % 8
                 a_copy(r, slot, slot).wait_recv()
 
-        def tile(n, _):
-            cols = pl.ds(pl.multiple_of(h * HALF + n * 256, 256), 256)
+        belongs = [cluster[0, zl * 8 + s] for s in range(8)]
+        for n in range(WIDE // 256):
+            cols = pl.ds(pl.multiple_of(h * WIDE + n * 256, 256), 256)
             nums = [jnp.zeros((16, 256), f32)] * CLUSTERS
             dens = [jnp.zeros((16, 256), f32)] * CLUSTERS
             for s in range(8):
                 a = a_recv[s, rows, cols].astype(f32)
                 aw = a * w_recv[s, rows, cols].astype(f32)
                 for k in range(CLUSTERS):
-                    member = mask[zl * 8 + s, k]
+                    member = jnp.where(belongs[s] == k, 1.0, 0.0)
                     nums[k] = nums[k] + member * aw
                     dens[k] = dens[k] + member * a
             for k in range(CLUSTERS):
                 num[k, rows, cols] = nums[k]
                 den[k, rows, cols] = dens[k]
-            return 0
-
-        lax.fori_loop(0, HALF // 256, tile, 0)
 
     def columns(way, h):
-        return pl.ds(pl.multiple_of(h * HALF + way * QUART, QUART), QUART)
-
-    def m_copy(way, j, peer):
-        return rcopy(m_send.at[way, j], m_recv.at[way, j], c_s.at[way, j, 0], c_r.at[way, j, 0], peer)
-
-    def d_copy(way, j, peer):
-        return rcopy(d_send.at[way, j], d_recv.at[way, j], c_s.at[way, j, 1], c_r.at[way, j, 1], peer)
+        return pl.ds(pl.multiple_of(h * WIDE + way * HALF, HALF), HALF)
+
+    def c_copy(way, j, peer):
+        return rcopy(c_send.at[way, j], c_recv.at[way, j], c_s.at[way], c_r.at[way, j], peer)
 
     def b_copy(way, j, peer):
         rows, _, h = where(j)
         part = merged.at[:, rows, columns(way, h)]
-        return rcopy(part, part, b_s.at[way, j], b_r.at[way, j], peer)
+        return rcopy(part, part, b_s.at[way], b_r.at[way, j], peer)
 
     def ends(way):
         if way == 0:
@@ -259,7 +277,7 @@
 
     def chain(way, i):
         hop, ahead, behind = ends(way)
-        j = i - hop
+        j = i - LAG * hop
 
         @pl.when((j >= 0) & (j < NS))
         def _():
@@ -268,23 +286,23 @@
 
             @pl.when(hop > 0)
             def _():
-                m_copy(way, j, behind).wait_recv()
-                d_copy(way, j, behind).wait_recv()
+                c_copy(way, j, behind).wait_recv()
                 for k in range(CLUSTERS):
-                    d = d_recv[way, j, k].astype(f32)
-                    v = m_recv[way, j, k].astype(jnp.int32).astype(f32) * (1.0 / CODE)
+                    v = c_recv[way, j, k].astype(jnp.int32).astype(f32) * (1.0 / CODE)
+                    e = c_recv[way, j, CLUSTERS + k].astype(jnp.int32)
+                    d = jnp.where(e < -32000, 0.0, jnp.exp(e.astype(f32) * STEP + MID))
                     num[k, rows, cols] += v * d
                     den[k, rows, cols] += d
 
             @pl.when(hop < 3)
             def _():
                 for k in range(CLUSTERS):
-                    d = den[k, rows, cols]
-                    v = num[k, rows, cols] / jnp.maximum(d, 0.0625)
-                    m_send[way, j, k] = jnp.round(v * CODE).astype(jnp.int32).astype(jnp.int16)
-                    d_send[way, j, k] = d.astype(bf16)
-                m_copy(way, j, ahead).start()
-                d_copy(way, j, ahead).start()
+                    d = jnp.maximum(den[k, rows, cols], LOW)
+                    v = num[k, rows, cols] / d
+                    e = (jnp.log(d) - MID) * (1.0 / STEP)
+                    c_send[way, j, k] = jnp.round(v * CODE).astype(jnp.int32).astype(jnp.int16)
+                    c_send[way, j, CLUSTERS + k] = jnp.round(e).astype(jnp.int32).astype(jnp.int16)
+                c_copy(way, j, ahead).start()
 
             @pl.when(hop == 3)
             def _():
@@ -294,7 +312,7 @@
 
     def back(way, i):
         hop, ahead, behind = ends(way)
-        j = i - (6 - hop)
+        j = i - LAG * (6 - hop)
 
         @pl.when((j >= 0) & (j < NS) & (hop < 3))
         def _():
@@ -306,22 +324,26 @@
 
     def o_copy(j, k, owner):
         rows, r, h = where(j)
-        cols = pl.ds(pl.multiple_of(h * HALF, HALF), HALF)
+        cols = pl.ds(pl.multiple_of(h * WIDE, WIDE), WIDE)
         dst = out.at[pl.ds(pl.multiple_of(owner * OWN + r * 16, 16), 16), cols]
-        return rcopy(picked.at[k, rows, cols], dst, o_s.at[k, j], o_r.at[owner, j], plane(k))
+        return rcopy(picked.at[k, rows, cols], dst, o_s.at[k], o_r.at[owner], plane(k))
+
+    def o_all(k, owner):
+        dst = out.at[pl.ds(pl.multiple_of(owner * OWN, 16), OWN)]
+        return rcopy(picked.at[k], dst, o_s.at[k], o_r.at[owner], plane(k))
 
     def l_copy(j):
         rows, r, h = where(j)
-        cols = pl.ds(pl.multiple_of(h * HALF, HALF), HALF)
+        cols = pl.ds(pl.multiple_of(h * WIDE, WIDE), WIDE)
         dst = out.at[pl.ds(pl.multiple_of(q * OWN + r * 16, 16), 16), cols]
-        return pltpu.make_async_copy(picked.at[q, rows, cols], dst, l_s.at[j])
+        return pltpu.make_async_copy(picked.at[q, rows, cols], dst, l_s.at[0])
 
     def scatter(j):
         rows, _, h = where(j)
-        cols = pl.ds(pl.multiple_of(h * HALF, HALF), HALF)
+        cols = pl.ds(pl.multiple_of(h * WIDE, WIDE), WIDE)
         for k in range(8):
             peer = (q + k) % 8
-            own_cluster = cluster[zl * 8 + peer, 0]
+            own_cluster = cluster[0, zl * 8 + peer]
             v = merged[0, rows, cols]
             for n in range(1, CLUSTERS):
                 v = jnp.where(own_cluster == n, merged[n, rows, cols], v)
@@ -331,47 +353,38 @@
             else:
                 o_copy(j, peer, q).start()
 
+    own_sums(0)
+
     def merge_step(i, _):
-        pl.when(i < NS)(lambda: own_sums(i))
         chain(0, i)
         chain(1, i)
         back(0, i)
         back(1, i)
-        pl.when(i >= 6)(lambda: scatter(i - 6))
-        return 0
-
-    lax.fori_loop(0, NS + 6, merge_step, 0)
-
-    def last_out(j, _):
-        l_copy(j).wait()
-        for k in range(1, 8):
-            peer = (q + k) % 8
-            o_copy(j, peer, peer).wait_recv()
-            o_copy(j, peer, q).wait_send()
-        for way in range(2):
-            hop, ahead, behind = ends(way)
-
-            @pl.when(hop < 3)
-            def _():
-                m_copy(way, j, ahead).wait_send()
-                d_copy(way, j, ahead).wait_send()
-
-            @pl.when(hop > 0)
-            def _():
-                b_copy(way, j, behind).wait_send()
-        return 0
-
-    lax.fori_loop(0, NS, last_out, 0)
-
-    def last_a(r, _):
-        for k in range(1, 8):
-            a_copy(r, (q + k) % 8, q).wait_send()
-        return 0
-
-    lax.fori_loop(0, NG, last_a, 0)
-    for k in range(1, 8):
-        w_copy((q + k) % 8, q).wait_send()
+        pl.when(i >= 6 * LAG)(lambda: scatter(i - 6 * LAG))
+        pl.when(i + 1 < NS)(lambda: own_sums(i + 1))
+        return 0
+
+    lax.fori_loop(0, NS + 6 * LAG, merge_step, 0)
+
+    for k in range(1, 8):
+        peer = (q + k) % 8
+        o_all(peer, peer).wait_recv()
+        o_all(peer, q).wait_send()
+        rcopy(a_send.at[pl.ds(pl.multiple_of(peer * OWN, 16), OWN)], a_recv.at[q], a_s.at[peer], a_r.at[q, 0], plane(peer)).wait_send()
+        w_copy(peer, q).wait_send()
         t_copy((m + k) % 8, m).wait_send()
+    pltpu.make_async_copy(picked.at[q], out.at[pl.ds(pl.multiple_of(q * OWN, 16), OWN)], l_s.at[0]).wait()
+    for way in range(2):
+        hop, ahead, behind = ends(way)
+
+        @pl.when(hop < 3)
+        def _():
+            rcopy(c_send.at[way], c_recv.at[way], c_s.at[way], c_r.at[way, 0], ahead).wait_send()
+
+        @pl.when(hop > 0)
+        def _():
+            part = merged.at[:, :, pl.ds(way * (D // 2), D // 2)]
+            rcopy(part, part, b_s.at[way], b_r.at[way, 0], behind).wait_send()
 
     def last_mp(b, _):
         for k in range(1, 4):
@@ -385,18 +398,19 @@
 
 
 def body(hidden, weight, target, router_prob, routes, assign):
-    token_weight = jnp.where(jnp.any(routes[0] == 0, axis=-1), router_prob[0], 0.0)
-    token_weight = jnp.broadcast_to(token_weight[:, :, None], (NB, 16, 128))
-    member = (assign == jnp.arange(CLUSTERS)[None, :]).astype(f32)
     vmem = pl.BlockSpec(memory_space=pltpu.VMEM)
     smem = pl.BlockSpec(memory_space=pltpu.SMEM)
+    hbm = pl.BlockSpec(memory_space=pl.ANY)
     V, S = pltpu.VMEM, pltpu.SemaphoreType.DMA
     result = pl.pallas_call(
         kernel,
         out_shape=jax.ShapeDtypeStruct((F, D), bf16),
-        in_specs=[vmem, vmem, vmem, vmem, smem, smem],
-        out_specs=pl.BlockSpec(memory_space=pl.ANY),
+        in_specs=[hbm, hbm, vmem, vmem, vmem, smem],
+        out_specs=hbm,
         scratch_shapes=[
+            V((NB, TOK, F), bf16),
+            V((F, D), bf16),
+            V((NB, 16, 128), f32),
             V((NB, F, TOK), bf16),
             V((TOK, D), f32),
             V((NB, 32, D), f32),
@@ -412,29 +426,28 @@
             V((8, OWN, D), bf16),
             V((CLUSTERS, OWN, D), f32),
             V((CLUSTERS, OWN, D), f32),
-            V((2, NS, CLUSTERS, G16, QUART), jnp.int16),
-            V((2, NS, CLUSTERS, G16, QUART), bf16),
-            V((2, NS, CLUSTERS, G16, QUART), jnp.int16),
-            V((2, NS, CLUSTERS, G16, QUART), bf16),
+            V((2, NS, 2 * CLUSTERS, G16, HALF), jnp.int16),
+            V((2, NS, 2 * CLUSTERS, G16, HALF), jnp.int16),
             V((CLUSTERS, OWN, D), bf16),
             V((8, OWN, D), bf16),
+            S((2,)),
             S((8,)), S((8,)),
             S((NB, 4)), S((NB, 4)),
             S((NB,)), S((NB,)),
             S((NB,)), S((NB,)),
             S((NB, 4)), S((NB, 4)),
             S((8,)), S((8,)),
-            S((8, NG)), S((8, NG)),
-            S((2, NS, 2)), S((2, NS, 2)),
-            S((2, NS)), S((2, NS)),
-            S((8, NS)), S((8, NS)),
-            S((NS,)),
+            S((8,)), S((8, NG)),
+            S((2,)), S((2, NS)),
+            S((2,)), S((2, NS)),
+            S((8,)), S((8,)),
+            S((1,)),
         ],
         compiler_params=pltpu.CompilerParams(
             collective_id=0, has_side_effects=True, vmem_limit_bytes=62 << 20
         ),
         cost_estimate=pl.CostEstimate(flops=4_000_000_000, bytes_accessed=12_000_000, transcendentals=0),
-    )(hidden[0], weight[0], target[0], token_weight, member, assign)
+    )(hidden[0], weight[0], target[0], router_prob[0], routes[0].transpose(0, 2, 1), assign.reshape(1, -1))
     return result[None]
 
 

time: 182 us -> 163 us (0.90)
  Pallas kernels: 172 us -> 159 us
  other arithmetic: 2.71 us -> 0 us
  local copies, waits for them, and re-layouts: 6.39 us -> 4.37 us
    pallas_call x1, Pallas kernels: 172 us -> 159 us  [body(): pl.pallas_call(kernel, out_shape=jax.ShapeDtypeStruct((F, D), bf16), in_s...]
    unnamed x2 -> x1, local copies, waits for them, and re-layouts: 5.71 us -> 4.37 us
where the time goes in v2:
time: 163 us
  Pallas kernels  159 us (98%)
  local copies, waits for them, and re-layouts  4.37 us (3%)
    pallas_call x1, Pallas kernels, body(): pl.pallas_call(kernel, out_shape=jax.ShapeDtypeStruct((F, D), bf16), in_s...  159 us
    unnamed x1, local copies, waits for them, and re-layouts  4.37 us

profile of v2, /device:TPU:1, one launch (start us, length us, event | category | flops | bytes accessed | tf_op | source)
XLA Modules:
  0.0 163.3 jit_solution(10822149758553816091)
XLA Ops:
  0.0 158.9 %shard_map.64 = bf16[896,2048]{1,0:T(8,128)(2,1)} custom-call(bf16[4,128,896]{2,1,0:T(8,128)(2,1)} %bitcast.11, bf16[896,2048]{1,0:T(8,128)(2,1)} %bitcast.10, bf16[4,16,2048]{2,1,0:T(8,128)(2,1)} %bitcast.12, f32[4,16]{1,0:T(4,128)} %bitcast.14, s32[4,2,16]{2,1,0:T(2,128)} %bitcast.13, s32[1,32]{1,0:T(1,128)} %bitcast.15), custom_call_target="tpu_custom_call" | custom-call | flops 4000000000 | bytes 12000000 | tf_op jit(solution)/shard_map/pallas_call | solution.py:405
  158.9 4.4 %copy.11 = bf16[1,896,2048]{2,1,0:T(8,128)(2,1)} copy(bf16[1,896,2048]{2,1,0:T(8,128)(2,1)} %bitcast.9) | data formatting | bytes 7340032

commit v3 on v2

--- a/solution.py
+++ b/solution.py
@@ -44,9 +44,9 @@
 
 def kernel(
     hid_in, w_in, tgt, prob, routes, cluster, out,
-    hid, w, tw, hid_t, y_f32, own, y_send, y_recv, z_send, z_recv, grad_out, fisher, sums, a_send, a_recv, w_recv,
+    hid, w, tw, hid_t, y_all, y_send, y_half, y_full, z_send, z_recv, grad_out, fisher, gram, sums, a_send, a_recv, w_recv,
     num, den, c_send, c_recv, merged, picked,
-    in_s, w_s, w_r, y_s, y_r, z_s, z_r, zg_s, zg_r, xg_s, xg_r, t_s, t_r, a_s, a_r, c_s, c_r, b_s, b_r, o_s, o_r, l_s,
+    in_s, w_s, w_r, yh_s, yh_r, yf_s, yf_r, z_s, z_r, zg_s, zg_r, xg_s, xg_r, xh_s, xh_r, t_s, t_r, a_s, a_r, f_r, c_s, c_r, b_s, b_r, o_s, o_r, l_s,
 ):
     c = lax.axis_index("client")
     m = lax.axis_index("mp")
@@ -87,51 +87,58 @@
         rows = pl.ds(pl.multiple_of(k * OWN, 16), OWN)
         return rcopy(w.at[rows], w_recv.at[slot], w_s.at[k], w_r.at[slot], plane(k))
 
-    def y_copy(b, k, slot):
-        rows = pl.ds(pl.multiple_of(k * 32, 32), 32)
+    right, left, opposite = (xx + 1) % 4, (xx + 3) % 4, (xx + 2) % 4
+    side = [group(right * 2 + zh), group(left * 2 + zh)]
+
+    def block(k):
+        return pl.ds(pl.multiple_of(k * 32, 32), 32)
+
+    def half(k, h):
+        return pl.ds(pl.multiple_of(k * 32 + h * 16, 16), 16)
+
+    def yh_copy(b, h):
+        return rcopy(y_send.at[b, half(opposite, h)], y_half.at[b, h], yh_s.at[b, h], yh_r.at[b, h], side[h])
+
+    def yf_copy(b, h):
         return rcopy(
-            y_send.at[b, rows], y_recv.at[b, slot], y_s.at[b, k], y_r.at[b, slot], group(k * 2 + zh)
+            y_send.at[b, block((right, left)[h])], y_full.at[b, h], yf_s.at[b, h], yf_r.at[b, h], side[h]
         )
 
-    def y_batch(b, _):
+    def step_y(b):
         for n in range(4):
             cols = pl.ds(n * QUART, QUART)
-            y_f32[:, cols] = jnp.dot(hid[b], w[:, cols], preferred_element_type=f32)
-            y_send[b, :, cols] = y_f32[:, cols].astype(bf16)
-        own[b] = y_f32[pl.ds(pl.multiple_of(xx * 32, 32), 32), :]
+            y_all[b, :, cols] = jnp.dot(hid[b], w[:, cols], preferred_element_type=f32)
+        y_send[b, block(opposite)] = y_all[b, block(opposite)].astype(bf16)
 
         @pl.when(b == 0)
         def _():
             pl.semaphore_wait(barrier, 16)
 
-        for k in range(1, 4):
-            y_copy(b, (xx + k) % 4, xx).start()
-        return 0
-
-    lax.fori_loop(0, NB, y_batch, 0)
-
-    for k in range(1, 8):
-        w_copy((q + k) % 8, q).start()
-
-    def prepare(b, _):
+        for h in range(2):
+            yh_copy(b, h).start()
+
+    def step_r(b):
+        for h in range(2):
+            k = (right, left)[h]
+            y_send[b, half(k, 1 - h)] = y_all[b, half(k, 1 - h)].astype(bf16)
+            yh_copy(b, h).wait_recv()
+            y_send[b, half(k, h)] = (y_all[b, half(k, h)] + y_half[b, h].astype(f32)).astype(bf16)
+            yf_copy(b, h).start()
+
+    def prepare(b):
         hid_t[b] = hid[b].T
-        return 0
-
-    lax.fori_loop(0, NB, prepare, 0)
-
-    def clear(r, _):
-        rows = pl.ds(pl.multiple_of(r * 16, 16), 16)
-        fisher[rows] = jnp.zeros((16, D), f32)
-        return 0
-
-    lax.fori_loop(0, F // 16, clear, 0)
-    sums[m] = jnp.zeros((8, 256), f32)
-
-    def keep_w(r, _):
-        w_recv[q, pl.ds(pl.multiple_of(r * 16, 16), 16)] = w[pl.ds(pl.multiple_of(q * OWN + r * 16, 16), 16)]
-        return 0
-
-    lax.fori_loop(0, NG, keep_w, 0)
+        gram[b] = lax.dot_general(hid[b], hid[b], (((1,), (1,)), ((), ())), preferred_element_type=f32)
+        fisher[pl.ds(pl.multiple_of(b * (F // NB), 32), F // NB)] = jnp.zeros((F // NB, D), f32)
+
+        @pl.when(b == 0)
+        def _():
+            sums[m] = jnp.zeros((8, 128), f32)
+            for k in range(1, 8):
+                w_copy((q + k) % 8, q).start()
+
+        @pl.when(b == 1)
+        def _():
+            w_recv[q] = w[pl.ds(pl.multiple_of(q * OWN, 16), OWN)]
 
     mine = pl.ds(pl.multiple_of(m * 16, 16), 16)
     theirs = pl.ds(pl.multiple_of((xx * 2 + 1 - zh) * 16, 16), 16)
@@ -143,62 +150,77 @@
     def zg_copy(b, rows):
         return rcopy(grad_out.at[b, rows], grad_out.at[b, rows], zg_s.at[b], zg_r.at[b], partner)
 
-    def xg_copy(b, k, block):
-        rows = pl.ds(pl.multiple_of(block * 32, 32), 32)
-        return rcopy(
-            grad_out.at[b, rows], grad_out.at[b, rows], xg_s.at[b, k], xg_r.at[b, block], group(k * 2 + zh)
-        )
+    def xg_copy(b, h, k):
+        part = grad_out.at[b, block(k)]
+        return rcopy(part, part, xg_s.at[b, h], xg_r.at[b, h], side[h])
+
+    def xh_copy(b, h, k):
+        part = grad_out.at[b, half(k, h)]
+        return rcopy(part, part, xh_s.at[b, h], xh_r.at[b, h], side[h])
 
     def step_x(b):
-        total = own[b]
-        for k in range(1, 4):
-            slot = (xx + k) % 4
-            y_copy(b, slot, slot).wait_recv()
-            total = total + y_recv[b, slot].astype(f32)
-        own[b] = total
-        z_send[b] = own[b, pl.ds(pl.multiple_of((1 - zh) * 16, 16), 16)].astype(bf16)
+        for h in range(2):
+            yf_copy(b, h).wait_recv()
+        z_send[b] = (
+            y_all[b, theirs] + y_full[b, 0, half(0, 1 - zh)].astype(f32) + y_full[b, 1, half(0, 1 - zh)].astype(f32)
+        ).astype(bf16)
         z_copy(b).start()
 
     def step_z(b):
+        y = y_all[b, mine] + y_full[b, 0, half(0, zh)].astype(f32) + y_full[b, 1, half(0, zh)].astype(f32)
         z_copy(b).wait_recv()
-        y = own[b, pl.ds(pl.multiple_of(zh * 16, 16), 16)] + z_recv[b].astype(f32)
+        y = y + z_recv[b].astype(f32)
         grad_out[b, mine] = (tw[b][:, :1] * (y - tgt[b].astype(f32))).astype(bf16)
         zg_copy(b, mine).start()
 
     def step_g(b):
         zg_copy(b, theirs).wait_recv()
-        for k in range(1, 4):
-            xg_copy(b, (xx + k) % 4, xx).start()
+        for h in range(2):
+            xg_copy(b, h, xx).start()
+
+    def step_h(b):
+        for h in range(2):
+            k = (left, right)[h]
+            xg_copy(b, h, k).wait_recv()
+            xh_copy(b, h, k).start()
+
+    def t_copy(k, slot):
+        return rcopy(sums.at[slot], sums.at[slot], t_s.at[k], t_r.at[slot], group(k))
 
     def step_f(b):
-        for k in range(1, 4):
-            slot = (xx + k) % 4
-            xg_copy(b, slot, slot).wait_recv()
+        for h in range(2):
+            xh_copy(b, h, opposite).wait_recv()
+        tokens = lax.dot_general(
+            grad_out[b], grad_out[b], (((1,), (1,)), ((), ())), preferred_element_type=f32
+        )
+        sums[m] += (tokens * gram[b]).reshape(TOK // 8, 8, TOK).sum(0)
+
+        @pl.when(b == NB - 1)
+        def _():
+            for k in range(1, 8):
+                t_copy((m + k) % 8, m).start()
 
         def tile(n, _):
             cols = pl.ds(pl.multiple_of(n * 256, 256), 256)
             g = jnp.dot(hid_t[b], grad_out[b, :, cols], preferred_element_type=f32)
-            g = g * g
-            fisher[:, cols] += g
-            sums[m] += g.reshape(F // 8, 8, 256).sum(0)
+            fisher[:, cols] += g * g
             return 0
 
         lax.fori_loop(0, D // 256, tile, 0)
 
     def mp_step(t, _):
-        pl.when(t < NB)(lambda: step_x(t))
-        pl.when((t >= 1) & (t < NB + 1))(lambda: step_z(t - 1))
-        pl.when((t >= 2) & (t < NB + 2))(lambda: step_g(t - 2))
-        pl.when(t >= 3)(lambda: step_f(t - 3))
+        pl.when(t < NB)(lambda: step_y(t))
+        pl.when((t >= 1) & (t < NB + 1))(lambda: step_r(t - 1))
+        pl.when((t >= 2) & (t < NB + 2))(lambda: step_x(t - 2))
+        pl.when((t >= 3) & (t < NB + 3))(lambda: step_z(t - 3))
+        pl.when((t >= 4) & (t < NB + 4))(lambda: step_g(t - 4))
+        pl.when((t >= 5) & (t < NB + 5))(lambda: step_h(t - 5))
+        pl.when(t < NB)(lambda: prepare(t))
+        pl.when(t >= 6)(lambda: step_f(t - 6))
         return 0
 
-    lax.fori_loop(0, NB + 3, mp_step, 0)
-
-    def t_copy(k, slot):
-        return rcopy(sums.at[slot], sums.at[slot], t_s.at[k], t_r.at[slot], group(k))
-
-    for k in range(1, 8):
-        t_copy((m + k) % 8, m).start()
+    lax.fori_loop(0, NB + 6, mp_step, 0)
+
     for k in range(1, 8):
         slot = (m + k) % 8
         t_copy(slot, slot).wait_recv()
@@ -214,7 +236,7 @@
         dst = pl.ds(pl.multiple_of(r * 16, 16), 16)
         return rcopy(a_send.at[src], a_recv.at[slot, dst], a_s.at[k], a_r.at[slot, r], plane(k))
 
-    def a_group(r, _):
+    def a_group(r):
         for k in range(1, 8):
             peer = (q + k) % 8
             rows = pl.ds(pl.multiple_of(peer * OWN + r * 16, 16), 16)
@@ -222,9 +244,20 @@
             a_copy(r, peer, q).start()
         rows = pl.ds(pl.multiple_of(q * OWN + r * 16, 16), 16)
         a_recv[q, pl.ds(pl.multiple_of(r * 16, 16), 16)] = (fisher[rows] * scale + FLOOR).astype(bf16)
-        return 0
-
-    lax.fori_loop(0, NG, a_group, 0)
+
+    def f_copy(h, k, slot):
+        cols = pl.ds(h * WIDE, WIDE)
+        src = a_send.at[pl.ds(pl.multiple_of(k * OWN, 16), 16), cols]
+        return rcopy(src, a_recv.at[slot, pl.ds(0, 16), cols], a_s.at[k], f_r.at[slot, h], plane(k))
+
+    for h in range(SPLIT):
+        cols = pl.ds(h * WIDE, WIDE)
+        for k in range(1, 8):
+            peer = (q + k) % 8
+            rows = pl.ds(pl.multiple_of(peer * OWN, 16), 16)
+            a_send[rows, cols] = (fisher[rows, cols] * scale + FLOOR).astype(bf16)
+            f_copy(h, peer, q).start()
+        a_recv[q, :16, cols] = (fisher[pl.ds(pl.multiple_of(q * OWN, 16), 16), cols] * scale + FLOOR).astype(bf16)
 
     for k in range(1, 8):
         slot = (q + k) % 8
@@ -237,7 +270,15 @@
     def own_sums(j):
         rows, r, h = where(j)
 
-        @pl.when(h == 0)
+        for piece in range(SPLIT):
+
+            @pl.when(j == piece)
+            def _():
+                for k in range(1, 8):
+                    slot = (q + k) % 8
+                    f_copy(piece, slot, slot).wait_recv()
+
+        @pl.when((h == 0) & (r > 0))
         def _():
             for k in range(1, 8):
                 slot = (q + k) % 8
@@ -353,9 +394,11 @@
             else:
                 o_copy(j, peer, q).start()
 
+    a_group(1)
     own_sums(0)
 
     def merge_step(i, _):
+        pl.when((i % SPLIT == 0) & (i // SPLIT + 2 < NG))(lambda: a_group(i // SPLIT + 2))
         chain(0, i)
         chain(1, i)
         back(0, i)
@@ -387,14 +430,22 @@
             rcopy(part, part, b_s.at[way], b_r.at[way, 0], behind).wait_send()
 
     def last_mp(b, _):
-        for k in range(1, 4):
-            y_copy(b, (xx + k) % 4, xx).wait_send()
-            xg_copy(b, (xx + k) % 4, xx).wait_send()
+        for h in range(2):
+            yh_copy(b, h).wait_send()
+            yf_copy(b, h).wait_send()
+            xg_copy(b, h, xx).wait_send()
+            xh_copy(b, h, opposite).wait_send()
         z_copy(b).wait_send()
         zg_copy(b, mine).wait_send()
         return 0
 
     lax.fori_loop(0, NB, last_mp, 0)
+
+
+def store(src, dst, sem):
+    copy = pltpu.make_async_copy(src, dst, sem.at[0])
+    copy.start()
+    copy.wait()
 
 
 def body(hidden, weight, target, router_prob, routes, assign):
@@ -404,23 +455,24 @@
     V, S = pltpu.VMEM, pltpu.SemaphoreType.DMA
     result = pl.pallas_call(
         kernel,
-        out_shape=jax.ShapeDtypeStruct((F, D), bf16),
+        out_shape=pltpu.VMEM((F, D), bf16),
         in_specs=[hbm, hbm, vmem, vmem, vmem, smem],
-        out_specs=hbm,
+        out_specs=vmem,
         scratch_shapes=[
             V((NB, TOK, F), bf16),
             V((F, D), bf16),
             V((NB, 16, 128), f32),
             V((NB, F, TOK), bf16),
-            V((TOK, D), f32),
-            V((NB, 32, D), f32),
+            V((NB, TOK, D), f32),
             V((NB, TOK, D), bf16),
-            V((NB, 4, 32, D), bf16),
+            V((NB, 2, 16, D), bf16),
+            V((NB, 2, 32, D), bf16),
             V((NB, 16, D), bf16),
             V((NB, 16, D), bf16),
             V((NB, TOK, D), bf16),
             V((F, D), f32),
-            V((8, 8, 256), f32),
+            V((NB, TOK, TOK), f32),
+            V((8, 8, 128), f32),
             V((F, D), bf16),
             V((8, OWN, D), bf16),
             V((8, OWN, D), bf16),
@@ -432,19 +484,21 @@
             V((8, OWN, D), bf16),
             S((2,)),
             S((8,)), S((8,)),
-            S((NB, 4)), S((NB, 4)),
+            S((NB, 2)), S((NB, 2)),
+            S((NB, 2)), S((NB, 2)),
             S((NB,)), S((NB,)),
             S((NB,)), S((NB,)),
-            S((NB, 4)), S((NB, 4)),
+            S((NB, 2)), S((NB, 2)),
+            S((NB, 2)), S((NB, 2)),
             S((8,)), S((8,)),
-            S((8,)), S((8, NG)),
+            S((8,)), S((8, NG)), S((8, SPLIT)),
             S((2,)), S((2, NS)),
             S((2,)), S((2, NS)),
             S((8,)), S((8,)),
             S((1,)),
         ],
         compiler_params=pltpu.CompilerParams(
-            collective_id=0, has_side_effects=True, vmem_limit_bytes=62 << 20
+            collective_id=0, has_side_effects=True, vmem_limit_bytes=58 << 20
         ),
         cost_estimate=pl.CostEstimate(flops=4_000_000_000, bytes_accessed=12_000_000, transcendentals=0),
     )(hidden[0], weight[0], target[0], router_prob[0], routes[0].transpose(0, 2, 1), assign.reshape(1, -1))

time: 163 us -> 158 us (0.969)
  Pallas kernels: 159 us -> 156 us
  local copies, waits for them, and re-layouts: 4.37 us -> 1.84 us
    pallas_call x1, Pallas kernels: 159 us -> 156 us  [body(): pl.pallas_call(kernel, out_shape=pltpu.VMEM((F, D), bf16), in_specs=[hbm,...]
    unnamed x1, local copies, waits for them, and re-layouts: 4.37 us -> 1.84 us
where the time goes in v3:
time: 158 us
  Pallas kernels  156 us (99%)
  local copies, waits for them, and re-layouts  1.84 us (1%)
    pallas_call x1, Pallas kernels, body(): pl.pallas_call(kernel, out_shape=pltpu.VMEM((F, D), bf16), in_specs=[hbm,...  156 us

profile of v3, /device:TPU:1, one launch (start us, length us, event | category | flops | bytes accessed | tf_op | source)
XLA Modules:
  0.0 157.7 jit_solution(8015262278470107713)
XLA Ops:
  0.0 155.8 %shard_map.64 = bf16[896,2048]{1,0:T(8,128)(2,1)S(1)} custom-call(bf16[4,128,896]{2,1,0:T(8,128)(2,1)} %bitcast.11, bf16[896,2048]{1,0:T(8,128)(2,1)} %bitcast.10, bf16[4,16,2048]{2,1,0:T(8,128)(2,1)} %bitcast.12, f32[4,16]{1,0:T(4,128)} %bitcast.14, s32[4,2,16]{2,1,0:T(2,128)} %bitcast.13, s32[1,32]{1,0:T(1,128)} %bitcast.15), custom_call_target="tpu_custom_call" | custom-call | flops 4000000000 | bytes 12000000 | tf_op jit(solution)/shard_map/pallas_call | solution.py:456
  155.8 1.8 %copy.11 = bf16[1,896,2048]{2,1,0:T(8,128)(2,1)} copy(bf16[1,896,2048]{2,1,0:T(8,128)(2,1)S(1)} %bitcast.9) | data formatting | bytes 7340032
